TPU v7x, 32 devices: a whole 2x2x4 slice. The times are simulated.
32 devices in a mesh: seq: 8 (over z, y), head: 4 (over x, core).
Axes of the slice: x: 2, y: 2, z: 4, core: 2. Of those that a mesh axis runs over, the one named last changes fastest.
Arguments:
- queries: bfloat16 [8192, 512], P(('seq', 'head')), may hold values from -6 to 6
- key_rows: bfloat16 [8192, 128], P(('seq', 'head')), may hold values from -6 to 6
- value_rows: bfloat16 [8192, 128], P(('seq', 'head')), may hold values from -6 to 6
- out_grad: bfloat16 [8192, 512], P(('seq', 'head')), may hold values from -6 to 6
- doc_start: int32 [32], replicated, may hold values from 0 to 255
Outputs:
- outputs: bfloat16 [8192, 512], P(('seq', 'head'))
- query_grad: bfloat16 [8192, 512], P(('seq', 'head'))
- key_grad: bfloat16 [8192, 128], P(('seq', 'head'))
- value_grad: bfloat16 [8192, 128], P(('seq', 'head'))
Inputs may be any that keep to these rules, and one draw needn't show every extreme that they name: doc_start[c] is the position within span c of the first token of a new document.
All inputs are finite; a program needn't handle non-finite values.
Results may differ from a plain program's by a relative error of at most 0.0065.
Values may be sent and summed in bfloat16 or wider, within the bound.
No kernel may reach another device: no remote copies, remote signals or barrier semaphores. Data moves between devices by JAX's collectives and lax.ppermute only.
A program may use at most 128 MiB of HBM per device.

v0:
```python
import math
import jax
import jax.numpy as jnp
from jax import lax
from jax.sharding import PartitionSpec as P

HD = 128
GROUP = 4
SPANS_DEV = 4
masked_fill = -1e30


def passed_along(value, axis, steps):
    count = lax.axis_size(axis)
    first, last = (max(0, -steps), min(count, count - steps))
    return lax.ppermute(value, axis, [(source, source + steps) for source in range(first, last)])


def allowed_mask(
    first_row, row_count, key_count, halo_len, span_len, span_start, prev_begin, span_index
):
    row_pos = first_row + lax.broadcasted_iota(jnp.int32, (row_count, key_count), 0)
    col_pos = lax.broadcasted_iota(jnp.int32, (row_count, key_count), 1) - halo_len
    return (
        (col_pos <= row_pos)
        & ((col_pos >= span_start) | (span_start > row_pos))
        & (col_pos >= prev_begin - span_len)
        & ((col_pos >= 0) | (span_index > 0))
    )


def attend(query_rows, grad_rows, key_block, value_block, allowed, head_dim):
    score_scale = 1.0 / math.sqrt(head_dim)
    contract = (((2,), (2,)), ((0,), (0,)))
    forward = (((2,), (1,)), ((0,), (0,)))
    backward = (((1,), (1,)), ((0,), (0,)))
    scores = (
        lax.dot_general(query_rows, key_block, contract, preferred_element_type=jnp.float32)
        * score_scale
    )
    masked = jnp.where(allowed, scores, masked_fill)
    row_max = jnp.max(masked, axis=2, keepdims=True)
    exp_scores = jnp.where(allowed, jnp.exp(masked - row_max), 0.0)
    weights = exp_scores / jnp.sum(exp_scores, axis=2, keepdims=True)
    weights_low = weights.astype(jnp.bfloat16)
    result = lax.dot_general(
        weights_low, value_block, forward, preferred_element_type=jnp.float32
    ).astype(jnp.bfloat16)
    grad_weights = lax.dot_general(
        grad_rows, value_block, contract, preferred_element_type=jnp.float32
    )
    row_delta = jnp.sum(weights * grad_weights, axis=2, keepdims=True)
    grad_scores = (weights * (grad_weights - row_delta) * score_scale).astype(jnp.bfloat16)
    grad_query = lax.dot_general(
        grad_scores, key_block, forward, preferred_element_type=jnp.float32
    )
    grad_key = lax.dot_general(
        grad_scores, query_rows, backward, preferred_element_type=jnp.float32
    )
    grad_value = lax.dot_general(
        weights_low, grad_rows, backward, preferred_element_type=jnp.float32
    )
    return (result, grad_query, grad_key, grad_value)


def per_device(queries, key_rows, value_rows, out_grad, doc_start):
    tok_count = queries.shape[0]
    head_count = lax.axis_size("head")
    group_rows = tok_count * head_count
    span_len = group_rows // SPANS_DEV
    halo_len = span_len // 4
    half_len = span_len // 2
    rest_len = span_len - halo_len
    head_q, head_grad = (
        lax.all_to_all(queries, "head", split_axis=1, concat_axis=0, tiled=True),
        lax.all_to_all(out_grad, "head", split_axis=1, concat_axis=0, tiled=True),
    )
    full_k, full_v = (
        lax.all_gather(key_rows, "head", axis=0, tiled=True),
        lax.all_gather(value_rows, "head", axis=0, tiled=True),
    )
    column = lax.axis_index("head") // GROUP * HD
    head_k = lax.dynamic_slice_in_dim(full_k, column, HD, 1)
    head_v = lax.dynamic_slice_in_dim(full_v, column, HD, 1)
    query_3 = head_q.reshape(SPANS_DEV, span_len, HD)
    grad_3 = head_grad.reshape(SPANS_DEV, span_len, HD)
    keys_3 = head_k.reshape(SPANS_DEV, span_len, HD)
    values_3 = head_v.reshape(SPANS_DEV, span_len, HD)
    tail_k = keys_3[:, rest_len:]
    tail_v = values_3[:, rest_len:]
    edge_last_k, edge_last_v = passed_along(
        (tail_k[SPANS_DEV - 1], tail_v[SPANS_DEV - 1]), "seq", 1
    )
    edge_k = jnp.concatenate([edge_last_k[None], tail_k[: SPANS_DEV - 1]], axis=0)
    edge_v = jnp.concatenate([edge_last_v[None], tail_v[: SPANS_DEV - 1]], axis=0)
    key_block = jnp.concatenate([edge_k, keys_3], axis=1)
    value_block = jnp.concatenate([edge_v, values_3], axis=1)
    first_span = lax.axis_index("seq") * SPANS_DEV
    span_starts = lax.dynamic_slice_in_dim(doc_start, first_span, SPANS_DEV)
    before_start = lax.dynamic_slice_in_dim(doc_start, jnp.maximum(first_span - 1, 0), 1)
    prev_starts = jnp.concatenate([before_start, span_starts[: SPANS_DEV - 1]], axis=0)
    span_ids = first_span + jnp.arange(SPANS_DEV, dtype=jnp.int32)
    span_starts = span_starts.reshape(SPANS_DEV, 1, 1)
    prev_starts = prev_starts.reshape(SPANS_DEV, 1, 1)
    span_ids = span_ids.reshape(SPANS_DEV, 1, 1)
    grad_key = jnp.zeros((SPANS_DEV, halo_len + span_len, HD), jnp.float32)
    grad_value = jnp.zeros((SPANS_DEV, halo_len + span_len, HD), jnp.float32)
    results = []
    query_grads = []
    for block_index in range(2):
        first_row = block_index * half_len
        key_count = halo_len + first_row + half_len
        allowed = allowed_mask(
            first_row, half_len, key_count, halo_len, span_len, span_starts, prev_starts, span_ids
        )
        result, grad_query, part_key, part_value = attend(
            query_3[:, first_row : first_row + half_len],
            grad_3[:, first_row : first_row + half_len],
            key_block[:, :key_count],
            value_block[:, :key_count],
            allowed,
            HD,
        )
        results.append(result)
        query_grads.append(grad_query.astype(jnp.bfloat16))
        grad_key = grad_key.at[:, :key_count].add(part_key)
        grad_value = grad_value.at[:, :key_count].add(part_value)
    next_last_k, next_last_v = passed_along(
        (grad_key[0, :halo_len], grad_value[0, :halo_len]), "seq", -1
    )
    next_k = jnp.concatenate([grad_key[1:, :halo_len], next_last_k[None]], axis=0)
    next_v = jnp.concatenate([grad_value[1:, :halo_len], next_last_v[None]], axis=0)
    own_k = jnp.concatenate(
        [grad_key[:, halo_len : halo_len + rest_len], grad_key[:, halo_len + rest_len :] + next_k],
        axis=1,
    ).reshape(group_rows, HD)
    own_v = jnp.concatenate(
        [
            grad_value[:, halo_len : halo_len + rest_len],
            grad_value[:, halo_len + rest_len :] + next_v,
        ],
        axis=1,
    ).reshape(group_rows, HD)
    all_results = jnp.concatenate(results, axis=1).reshape(group_rows, HD)
    all_query_grads = jnp.concatenate(query_grads, axis=1).reshape(group_rows, HD)
    outputs, query_grad = (
        lax.all_to_all(all_results, "head", split_axis=0, concat_axis=1, tiled=True),
        lax.all_to_all(all_query_grads, "head", split_axis=0, concat_axis=1, tiled=True),
    )
    wide_gk, wide_gv = (
        lax.all_to_all(own_k, "head", split_axis=0, concat_axis=1, tiled=True),
        lax.all_to_all(own_v, "head", split_axis=0, concat_axis=1, tiled=True),
    )
    group_total = wide_gk.shape[1] // (GROUP * HD)
    key_grad = (
        wide_gk.reshape(tok_count, group_total, GROUP, HD)
        .sum(axis=2)
        .reshape(tok_count, group_total * HD)
        .astype(jnp.bfloat16)
    )
    value_grad = (
        wide_gv.reshape(tok_count, group_total, GROUP, HD)
        .sum(axis=2)
        .reshape(tok_count, group_total * HD)
        .astype(jnp.bfloat16)
    )
    return (outputs, query_grad, key_grad, value_grad)


def solution(mesh):
    placed = (
        P(("seq", "head"), None),
        P(("seq", "head"), None),
        P(("seq", "head"), None),
        P(("seq", "head"), None),
        P(),
    )
    return jax.shard_map(
        per_device,
        mesh=mesh,
        in_specs=placed,
        out_specs=(
            P(("seq", "head"), None),
            P(("seq", "head"), None),
            P(("seq", "head"), None),
            P(("seq", "head"), None),
        ),
        check_vma=False,
    )
```

profile of v0, /device:TPU:8, one launch (start us, length us, event | category | flops | bytes accessed | tf_op | source)
XLA Modules:
  0.0 94.2 jit_solution(2533710951645964501)
XLA Ops:
  0.6 6.1 %all_gather.7 = bf16[1024,128]{1,0:T(8,128)(2,1)S(1)} all-gather(bf16[256,128]{1,0:T(8,128)(2,1)} %param.19), channel_id=1, replica_groups=mesh['seq'=8,'head'=4] {'head'}, dimensions={0}, use_global_device_ids=true | all-gather | bytes 327680 | tf_op jit(solution)/shard_map/all_gather | solution.py:80
  6.8 3.5 %collective-permute-start.1 = (bf16[64,128]{1,0:T(8,128)(2,1)S(1)}, bf16[64,128]{1,0:T(8,128)(2,1)S(1)}, u32[]{:S(2)}, u32[]{:S(2)}) collective-permute-start(bf16[64,128]{1,0:T(8,128)(2,1)S(1)} %slice_bitcast_fusion.2), channel_id=1, source_target_pairs={{0,4},{4,8},{8,12},{12,16},{16,20},{20,24},{24,28},{1,5},{5,9},{9,... | collective-permute-start | bytes 49160 | tf_op jit(solution)/shard_map/ppermute | solution.py:16
  10.3 5.8 %all_gather.6 = bf16[1024,128]{1,0:T(8,128)(2,1)S(1)} all-gather(bf16[256,128]{1,0:T(8,128)(2,1)S(1)} %copy-done.2), channel_id=1, replica_groups=mesh['seq'=8,'head'=4] {'head'}, dimensions={0}, use_global_device_ids=true | all-gather | bytes 327680 | tf_op jit(solution)/shard_map/all_gather | solution.py:79
  16.1 3.4 %collective-permute-start = (bf16[64,128]{1,0:T(8,128)(2,1)S(1)}, bf16[64,128]{1,0:T(8,128)(2,1)S(1)}, u32[]{:S(2)}, u32[]{:S(2)}) collective-permute-start(bf16[64,128]{1,0:T(8,128)(2,1)S(1)} %slice_bitcast_fusion.3), channel_id=1, source_target_pairs={{0,4},{4,8},{8,12},{12,16},{16,20},{20,24},{24,28},{1,5},{5,9},{9,... | collective-permute-start | bytes 49160 | tf_op jit(solution)/shard_map/ppermute | solution.py:16
  20.6 3.5 %all-to-all-start.2 = ((bf16[256,4,128]{2,0,1:T(8,128)(2,1)}), bf16[256,4,128]{2,0,1:T(8,128)(2,1)S(1)}, u32[]{:S(2)}, u32[]{:S(2)}) async-start(bf16[256,4,128]{2,0,1:T(8,128)(2,1)} %copy.13), calls=%async_computation.2 | async-start | bytes 524288 | tf_op jit(solution)/shard_map/all_to_all | solution.py:76
  26.9 3.2 %all-to-all-done.2 = bf16[256,4,128]{2,0,1:T(8,128)(2,1)S(1)} async-done(((bf16[256,4,128]{2,0,1:T(8,128)(2,1)}), bf16[256,4,128]{2,0,1:T(8,128)(2,1)S(1)}, u32[]{:S(2)}, u32[]{:S(2)}) %all-to-all-start.2) | async-done | bytes 262176 | tf_op jit(solution)/shard_map/all_to_all | solution.py:76
  30.1 3.4 %all-to-all-start = ((bf16[256,4,128]{2,0,1:T(8,128)(2,1)}), bf16[256,4,128]{2,0,1:T(8,128)(2,1)S(1)}, u32[]{:S(2)}, u32[]{:S(2)}) async-start(bf16[256,4,128]{2,0,1:T(8,128)(2,1)} %copy.10), calls=%async_computation | async-start | bytes 524288 | tf_op jit(solution)/shard_map/all_to_all | solution.py:75
  34.0 5.5 %all-to-all-done = bf16[256,4,128]{2,0,1:T(8,128)(2,1)S(1)} async-done(((bf16[256,4,128]{2,0,1:T(8,128)(2,1)}), bf16[256,4,128]{2,0,1:T(8,128)(2,1)S(1)}, u32[]{:S(2)}, u32[]{:S(2)}) %all-to-all-start) | async-done | bytes 262176 | tf_op jit(solution)/shard_map/all_to_all | solution.py:75
  40.7 1.3 %fusion.43 = f32[4,192,128]{2,1,0:T(8,128)} fusion(bf16[4,256,128]{2,1,0:T(8,128)(2,1)S(1)} %bitcast.71, f32[4,128]{1,0:T(4,128)S(1)} %get-tuple-element.74, bf16[4,256,128]{2,1,0:T(8,128)(2,1)S(1)} %bitcast.91, bf16[4,256,128]{2,1,0:T(8,128)(2,1)S(1)} %bitcast.83, bf16[3,64,128]{2,1,0:T(8,128)(2,1)S(1)} %slice.163, bf16[1,64,128]{2,1,0:T(8,128)(2,1)S(1)} %bitcast.105, ...), kind=kOutput, calls=%fused_computation.65 | convolution fusion | flops 53084864 | bytes 1040384 | tf_op jit(solution)/shard_map/dot_general | solution.py:60
  42.0 1.5 %fusion.103 = (f32[4,128]{1,0:T(4,128)S(1)}, f32[4,128,320]{1,2,0:T(8,128)}) fusion(bf16[4,256,128]{2,1,0:T(8,128)(2,1)S(1)} %bitcast.84, bf16[3,64,128]{2,1,0:T(8,128)(2,1)S(1)} %slice.163, bf16[1,64,128]{2,1,0:T(8,128)(2,1)S(1)} %bitcast.106, bf16[4,256,128]{2,1,0:T(8,128)(2,1)S(1)} %bitcast.92, pred[4]{0:T(512)(128)(4,1)S(1)} %add_compare_fusion, ...), kind=kOutput, calls=%fused_computation.111 | convolution fusion | flops 46367040 | bytes 1207296 | tf_op jit(solution)/shard_map/sub | solution.py:43
  45.3 3.4 %all-to-all-start.1 = ((bf16[4,256,128]{2,1,0:T(8,128)(2,1)}), bf16[4,256,128]{2,1,0:T(8,128)(2,1)S(1)}, u32[]{:S(2)}, u32[]{:S(2)}) async-start(bf16[4,256,128]{2,1,0:T(8,128)(2,1)} %pad_maximum_fusion.4), calls=%async_computation.1 | async-start | bytes 524288 | tf_op jit(solution)/shard_map/all_to_all | solution.py:147
  48.7 1.7 %convolution_convert_fusion = bf16[4,128,128]{2,1,0:T(8,128)(2,1)S(1)} fusion(f32[4,128,320]{1,2,0:T(8,128)S(1)} %convolution_bitcast_fusion, bf16[4,256,128]{2,1,0:T(8,128)(2,1)S(1)} %bitcast.86, bf16[3,64,128]{2,1,0:T(8,128)(2,1)S(1)} %slice.163, bf16[1,64,128]{2,1,0:T(8,128)(2,1)S(1)} %bitcast.108, f32[4,128,320]{1,2,0:T(8,128)} %get-tuple-element.73, ...), kind=kOutput, calls=%fused_computation.28 | convolution fusion | flops 44139328 | bytes 1771520 | tf_op jit(solution)/shard_map/dot_general | solution.py:54
  50.4 1.0 %fusion.22 = f32[4,192,128]{2,1,0:T(8,128)} fusion(f32[4,128,192]{1,2,0:T(8,128)S(1)} %convolution_bitcast_fusion.1, bf16[4,256,128]{2,1,0:T(8,128)(2,1)S(1)} %bitcast.94, f32[4,128,192]{1,2,0:T(8,128)S(1)} %get-tuple-element.75, f32[4,128]{1,0:T(4,128)S(1)} %get-tuple-element.74), kind=kOutput, calls=%fused_computation.32 | convolution fusion | flops 25854656 | bytes 2101248 | tf_op jit(solution)/shard_map/dot_general | solution.py:57
  51.4 1.7 %convolution_add_fusion.1 = f32[4,320,128]{2,1,0:T(8,128)S(1)} fusion(f32[4,128,320]{1,2,0:T(8,128)S(1)} %convolution_bitcast_fusion, f32[4,192,128]{2,1,0:T(8,128)} %fusion.22, bf16[4,256,128]{2,1,0:T(8,128)(2,1)S(1)} %bitcast.95, f32[4,128,320]{1,2,0:T(8,128)} %get-tuple-element.73, f32[4,128]{1,0:T(4,128)S(1)} %get-tuple-element.72), kind=kOutput, calls=%fused_computation.11 | convolution fusion | flops 43254592 | bytes 3805184 | tf_op jit(solution)/shard_map/dot_general | solution.py:57
  53.2 3.3 %collective-permute-start.2 = (f32[64,128]{1,0:T(8,128)S(1)}, f32[64,128]{1,0:T(8,128)S(1)}, u32[]{:S(2)}, u32[]{:S(2)}) collective-permute-start(f32[64,128]{1,0:T(8,128)S(1)} %slice_bitcast_fusion.1), channel_id=1, source_target_pairs={{4,0},{8,4},{12,8},{16,12},{20,16},{24,20},{28,24},{5,1},{9,5},{13... | collective-permute-start | bytes 98312 | tf_op jit(solution)/shard_map/ppermute | solution.py:16
  56.6 1.9 %convolution_add_fusion = f32[4,320,128]{2,1,0:T(8,128)S(1)} fusion(f32[4,192,128]{2,1,0:T(8,128)} %fusion.43, bf16[4,256,128]{2,1,0:T(8,128)(2,1)S(1)} %bitcast.72, f32[4,128]{1,0:T(4,128)S(1)} %get-tuple-element.72, bf16[4,256,128]{2,1,0:T(8,128)(2,1)S(1)} %bitcast.87, bf16[3,64,128]{2,1,0:T(8,128)(2,1)S(1)} %copy-done.4, ...), kind=kOutput, calls=%fused_computation.10 | convolution fusion | flops 88638272 | bytes 1731584 | tf_op jit(solution)/shard_map/dot_general | solution.py:60
  59.6 3.4 %all-to-all-start.3 = ((bf16[4,256,128]{2,1,0:T(8,128)(2,1)}), bf16[4,256,128]{2,1,0:T(8,128)(2,1)S(1)}, u32[]{:S(2)}, u32[]{:S(2)}) async-start(bf16[4,256,128]{2,1,0:T(8,128)(2,1)} %pad_maximum_fusion.5), calls=%async_computation.3 | async-start | bytes 524288 | tf_op jit(solution)/shard_map/all_to_all | solution.py:148
  63.9 5.1 %all-to-all-done.3 = bf16[4,256,128]{2,1,0:T(8,128)(2,1)S(1)} async-done(((bf16[4,256,128]{2,1,0:T(8,128)(2,1)}), bf16[4,256,128]{2,1,0:T(8,128)(2,1)S(1)}, u32[]{:S(2)}, u32[]{:S(2)}) %all-to-all-start.3) | async-done | bytes 262176 | tf_op jit(solution)/shard_map/all_to_all | solution.py:148
  69.0 3.5 %all-to-all-start.4 = ((f32[4,256,128]{2,1,0:T(8,128)}), f32[4,256,128]{2,1,0:T(8,128)S(1)}, u32[]{:S(2)}, u32[]{:S(2)}) async-start(f32[4,256,128]{2,1,0:T(8,128)} %pad_maximum_fusion), calls=%async_computation.4 | async-start | bytes 1048576 | tf_op jit(solution)/shard_map/all_to_all | solution.py:151
  72.5 2.4 %collective-permute-start.3 = (f32[64,128]{1,0:T(8,128)S(1)}, f32[64,128]{1,0:T(8,128)S(1)}, u32[]{:S(2)}, u32[]{:S(2)}) collective-permute-start(f32[64,128]{1,0:T(8,128)S(1)} %slice_bitcast_fusion), channel_id=1, source_target_pairs={{4,0},{8,4},{12,8},{16,12},{20,16},{24,20},{28,24},{5,1},{9,5},{13... | collective-permute-start | bytes 98312 | tf_op jit(solution)/shard_map/ppermute | solution.py:16
  75.0 3.3 %collective-permute-done.3 = f32[64,128]{1,0:T(8,128)S(1)} collective-permute-done((f32[64,128]{1,0:T(8,128)S(1)}, f32[64,128]{1,0:T(8,128)S(1)}, u32[]{:S(2)}, u32[]{:S(2)}) %collective-permute-start.3) | collective-permute-done | bytes 32800 | tf_op jit(solution)/shard_map/ppermute | solution.py:16
  79.2 2.1 %all-to-all-done.4 = f32[4,256,128]{2,1,0:T(8,128)S(1)} async-done(((f32[4,256,128]{2,1,0:T(8,128)}), f32[4,256,128]{2,1,0:T(8,128)S(1)}, u32[]{:S(2)}, u32[]{:S(2)}) %all-to-all-start.4) | async-done | bytes 524320 | tf_op jit(solution)/shard_map/all_to_all | solution.py:151
  81.3 3.5 %all-to-all-start.5 = ((f32[4,256,128]{2,1,0:T(8,128)}), f32[4,256,128]{2,1,0:T(8,128)S(1)}, u32[]{:S(2)}, u32[]{:S(2)}) async-start(f32[4,256,128]{2,1,0:T(8,128)} %pad_maximum_fusion.1), calls=%async_computation.5 | async-start | bytes 1048576 | tf_op jit(solution)/shard_map/all_to_all | solution.py:152
  87.4 6.2 %all-to-all-done.5 = f32[4,256,128]{2,1,0:T(8,128)S(1)} async-done(((f32[4,256,128]{2,1,0:T(8,128)}), f32[4,256,128]{2,1,0:T(8,128)S(1)}, u32[]{:S(2)}, u32[]{:S(2)}) %all-to-all-start.5) | async-done | bytes 524320 | tf_op jit(solution)/shard_map/all_to_all | solution.py:152
  (73 shorter events, 13.1 us)
Async XLA Ops:
  0.6 9.7 %copy-start.2 = (bf16[256,128]{1,0:T(8,128)(2,1)S(1)}, bf16[256,128]{1,0:T(8,128)(2,1)}, u32[]{:S(2)}) copy-start(bf16[256,128]{1,0:T(8,128)(2,1)} %param.18) | copy-start | bytes 196612
  6.8 12.8 %copy-start = (bf16[256,512]{1,0:T(8,128)(2,1)S(1)}, bf16[256,512]{1,0:T(8,128)(2,1)}, u32[]{:S(2)}) copy-start(bf16[256,512]{1,0:T(8,128)(2,1)} %param.20) | copy-start | bytes 786436
  6.8 26.7 %collective-permute-start.1 = (bf16[64,128]{1,0:T(8,128)(2,1)S(1)}, bf16[64,128]{1,0:T(8,128)(2,1)S(1)}, u32[]{:S(2)}, u32[]{:S(2)}) collective-permute-start(bf16[64,128]{1,0:T(8,128)(2,1)S(1)} %slice_bitcast_fusion.2), channel_id=1, source_target_pairs={{0,4},{4,8},{8,12},{12,16},{16,20},{20,24},{24,28},{1,5},{5,9},{9,... | collective-permute-start | bytes 49160 | tf_op jit(solution)/shard_map/ppermute | solution.py:16
  16.1 17.9 %collective-permute-start = (bf16[64,128]{1,0:T(8,128)(2,1)S(1)}, bf16[64,128]{1,0:T(8,128)(2,1)S(1)}, u32[]{:S(2)}, u32[]{:S(2)}) collective-permute-start(bf16[64,128]{1,0:T(8,128)(2,1)S(1)} %slice_bitcast_fusion.3), channel_id=1, source_target_pairs={{0,4},{4,8},{8,12},{12,16},{16,20},{20,24},{24,28},{1,5},{5,9},{9,... | collective-permute-start | bytes 49160 | tf_op jit(solution)/shard_map/ppermute | solution.py:16
  20.5 3.7 %copy-start.8 = (s32[32]{0:T(128)S(1)}, s32[32]{0:T(128)}, u32[]{:S(2)}) copy-start(s32[32]{0:T(128)} %param.21) | copy-start | bytes 388
  20.6 9.5 %all-to-all-start.2 = ((bf16[256,4,128]{2,0,1:T(8,128)(2,1)}), bf16[256,4,128]{2,0,1:T(8,128)(2,1)S(1)}, u32[]{:S(2)}, u32[]{:S(2)}) async-start(bf16[256,4,128]{2,0,1:T(8,128)(2,1)} %copy.13), calls=%async_computation.2 | async-start | bytes 524288 | tf_op jit(solution)/shard_map/all_to_all | solution.py:76
  24.1 1.8 %copy-start.1 = (bf16[256,512]{1,0:T(8,128)(2,1)S(1)}, bf16[256,512]{1,0:T(8,128)(2,1)}, u32[]{:S(2)}) copy-start(bf16[256,512]{1,0:T(8,128)(2,1)} %param.17) | copy-start | bytes 786436
  24.1 19.4 %copy-start.11 = (pred[320]{0:T(512)(128)(4,1)}, pred[320]{0:T(512)(128)(4,1)S(1)}, u32[]{:S(2)}) copy-start(pred[320]{0:T(512)(128)(4,1)S(1)} %broadcast_compare_fusion.1) | copy-start | bytes 964
  24.2 19.4 %copy-start.9 = (pred[4]{0:T(512)(128)(4,1)}, pred[4]{0:T(512)(128)(4,1)S(1)}, u32[]{:S(2)}) copy-start(pred[4]{0:T(512)(128)(4,1)S(1)} %add_compare_fusion) | copy-start | bytes 16
  25.1 18.5 %copy-start.5 = (pred[128,320]{0,1:T(8,128)(4,1)}, pred[128,320]{0,1:T(8,128)(4,1)S(1)}, u32[]{:S(2)}) copy-start(pred[128,320]{0,1:T(8,128)(4,1)S(1)} %broadcast_compare_fusion) | copy-start | bytes 122884
  25.9 22.8 %copy-start.3 = (bf16[3,64,128]{2,1,0:T(8,128)(2,1)}, bf16[3,64,128]{2,1,0:T(8,128)(2,1)S(1)}, u32[]{:S(2)}) copy-start(bf16[3,64,128]{2,1,0:T(8,128)(2,1)S(1)} %slice.163) | copy-start | bytes 147460
  30.1 9.4 %all-to-all-start = ((bf16[256,4,128]{2,0,1:T(8,128)(2,1)}), bf16[256,4,128]{2,0,1:T(8,128)(2,1)S(1)}, u32[]{:S(2)}, u32[]{:S(2)}) async-start(bf16[256,4,128]{2,0,1:T(8,128)(2,1)} %copy.10), calls=%async_computation | async-start | bytes 524288 | tf_op jit(solution)/shard_map/all_to_all | solution.py:75
  34.0 14.7 %copy-start.6 = (bf16[64,128]{1,0:T(8,128)(2,1)}, bf16[64,128]{1,0:T(8,128)(2,1)S(1)}, u32[]{:S(2)}) copy-start(bf16[64,128]{1,0:T(8,128)(2,1)S(1)} %collective-permute-done) | copy-start | bytes 49156
  45.3 14.3 %all-to-all-start.1 = ((bf16[4,256,128]{2,1,0:T(8,128)(2,1)}), bf16[4,256,128]{2,1,0:T(8,128)(2,1)S(1)}, u32[]{:S(2)}, u32[]{:S(2)}) async-start(bf16[4,256,128]{2,1,0:T(8,128)(2,1)} %pad_maximum_fusion.4), calls=%async_computation.1 | async-start | bytes 524288 | tf_op jit(solution)/shard_map/all_to_all | solution.py:147
  51.4 5.1 %copy-start.10 = (pred[4]{0:T(512)(128)(4,1)S(1)}, pred[4]{0:T(512)(128)(4,1)}, u32[]{:S(2)}) copy-start(pred[4]{0:T(512)(128)(4,1)} %copy-done.9) | copy-start | bytes 16
  51.4 5.1 %copy-start.12 = (pred[320]{0:T(512)(128)(4,1)S(1)}, pred[320]{0:T(512)(128)(4,1)}, u32[]{:S(2)}) copy-start(pred[320]{0:T(512)(128)(4,1)} %copy-done.11) | copy-start | bytes 964
  53.2 3.4 %copy-start.4 = (bf16[3,64,128]{2,1,0:T(8,128)(2,1)S(1)}, bf16[3,64,128]{2,1,0:T(8,128)(2,1)}, u32[]{:S(2)}) copy-start(bf16[3,64,128]{2,1,0:T(8,128)(2,1)} %copy-done.3) | copy-start | bytes 147460
  53.2 3.4 %copy-start.7 = (bf16[64,128]{1,0:T(8,128)(2,1)S(1)}, bf16[64,128]{1,0:T(8,128)(2,1)}, u32[]{:S(2)}) copy-start(bf16[64,128]{1,0:T(8,128)(2,1)} %copy-done.6) | copy-start | bytes 49156
  53.2 9.8 %collective-permute-start.2 = (f32[64,128]{1,0:T(8,128)S(1)}, f32[64,128]{1,0:T(8,128)S(1)}, u32[]{:S(2)}, u32[]{:S(2)}) collective-permute-start(f32[64,128]{1,0:T(8,128)S(1)} %slice_bitcast_fusion.1), channel_id=1, source_target_pairs={{4,0},{8,4},{12,8},{16,12},{20,16},{24,20},{28,24},{5,1},{9,5},{13... | collective-permute-start | bytes 98312 | tf_op jit(solution)/shard_map/ppermute | solution.py:16
  59.6 9.4 %all-to-all-start.3 = ((bf16[4,256,128]{2,1,0:T(8,128)(2,1)}), bf16[4,256,128]{2,1,0:T(8,128)(2,1)S(1)}, u32[]{:S(2)}, u32[]{:S(2)}) async-start(bf16[4,256,128]{2,1,0:T(8,128)(2,1)} %pad_maximum_fusion.5), calls=%async_computation.3 | async-start | bytes 524288 | tf_op jit(solution)/shard_map/all_to_all | solution.py:148
  69.0 12.3 %all-to-all-start.4 = ((f32[4,256,128]{2,1,0:T(8,128)}), f32[4,256,128]{2,1,0:T(8,128)S(1)}, u32[]{:S(2)}, u32[]{:S(2)}) async-start(f32[4,256,128]{2,1,0:T(8,128)} %pad_maximum_fusion), calls=%async_computation.4 | async-start | bytes 1048576 | tf_op jit(solution)/shard_map/all_to_all | solution.py:151
  72.5 5.8 %collective-permute-start.3 = (f32[64,128]{1,0:T(8,128)S(1)}, f32[64,128]{1,0:T(8,128)S(1)}, u32[]{:S(2)}, u32[]{:S(2)}) collective-permute-start(f32[64,128]{1,0:T(8,128)S(1)} %slice_bitcast_fusion), channel_id=1, source_target_pairs={{4,0},{8,4},{12,8},{16,12},{20,16},{24,20},{28,24},{5,1},{9,5},{13... | collective-permute-start | bytes 98312 | tf_op jit(solution)/shard_map/ppermute | solution.py:16
  81.3 12.3 %all-to-all-start.5 = ((f32[4,256,128]{2,1,0:T(8,128)}), f32[4,256,128]{2,1,0:T(8,128)S(1)}, u32[]{:S(2)}, u32[]{:S(2)}) async-start(f32[4,256,128]{2,1,0:T(8,128)} %pad_maximum_fusion.1), calls=%async_computation.5 | async-start | bytes 1048576 | tf_op jit(solution)/shard_map/all_to_all | solution.py:152
where the time goes:
time: 95.1 us; the launch traced here: 94.2 us
  starting transfers between devices  33.4 us (35%)
  waiting for transfers between devices  25.5 us (27%)
  matrix products  12.1 us (13%)
  blocking collectives  11.9 us (13%)
  other arithmetic  5.42 us (6%)
  local copies, waits for them, and re-layouts  4.74 us (5%)
  between operations  1.09 us (1%)
    ppermute x4, starting transfers between devices, passed_along(): lax.ppermute(value, axis, [(source, source + steps) for source in range(f...  12.7 us
    all_to_all x1, waiting for transfers between devices, per_device(): lax.all_to_all(own_v, 'head', split_axis=0, concat_axis=1, tiled=True)  6.16 us
    all_gather x1, blocking collectives, per_device(): lax.all_gather(value_rows, 'head', axis=0, tiled=True)  6.13 us
    all_gather x1, blocking collectives, per_device(): lax.all_gather(key_rows, 'head', axis=0, tiled=True)  5.79 us
    all_to_all x1, waiting for transfers between devices, per_device(): lax.all_to_all(queries, 'head', split_axis=1, concat_axis=0, tiled=True)  5.5 us
    all_to_all x1, waiting for transfers between devices, per_device(): lax.all_to_all(all_query_grads, 'head', split_axis=0, concat_axis=1, tile...  5.14 us
    all_to_all x1, starting transfers between devices, per_device(): lax.all_to_all(out_grad, 'head', split_axis=1, concat_axis=0, tiled=True)  3.54 us
    all_to_all x1, starting transfers between devices, per_device(): lax.all_to_all(own_v, 'head', split_axis=0, concat_axis=1, tiled=True)  3.47 us
  transfers between devices with their start and end apart: 10, of which 6 were waited for; matrix products, arithmetic and copies ran while one was open for 17% of the time, Pallas kernels for 0%

commit v1 on v0

--- a/solution.py
+++ b/solution.py
@@ -144,7 +144,15 @@
     all_results = jnp.concatenate(results, axis=1).reshape(group_rows, HD)
     all_query_grads = jnp.concatenate(query_grads, axis=1).reshape(group_rows, HD)
     outputs, query_grad = (
-        lax.all_to_all(all_results, "head", split_axis=0, concat_axis=1, tiled=True),
+        jnp.concatenate(
+            jax.lax.all_to_all(
+                jnp.stack(jnp.split(all_results, jax.lax.axis_size("head"), axis=0), axis=0),
+                "head",
+                0,
+                0,
+            ),
+            axis=1,
+        ),
         lax.all_to_all(all_query_grads, "head", split_axis=0, concat_axis=1, tiled=True),
     )
     wide_gk, wide_gv = (

time: 95.1 us -> 95.1 us (level)
  no operation moved by 1% of the time
where the time goes in v1:
time: 95.1 us; the launch traced here: 94.2 us
  starting transfers between devices  33.4 us (35%)
  waiting for transfers between devices  25.5 us (27%)
  matrix products  12.1 us (13%)
  blocking collectives  11.9 us (13%)
  other arithmetic  5.42 us (6%)
  local copies, waits for them, and re-layouts  4.74 us (5%)
  between operations  1.09 us (1%)
    ppermute x4, starting transfers between devices, passed_along(): lax.ppermute(value, axis, [(source, source + steps) for source in range(f...  12.7 us
    all_to_all x1, waiting for transfers between devices, per_device(): lax.all_to_all(own_v, 'head', split_axis=0, concat_axis=1, tiled=True)  6.16 us
    all_gather x1, blocking collectives, per_device(): lax.all_gather(value_rows, 'head', axis=0, tiled=True)  6.13 us
    all_gather x1, blocking collectives, per_device(): lax.all_gather(key_rows, 'head', axis=0, tiled=True)  5.79 us
    all_to_all x1, waiting for transfers between devices, per_device(): lax.all_to_all(queries, 'head', split_axis=1, concat_axis=0, tiled=True)  5.5 us
    all_to_all x1, waiting for transfers between devices, per_device(): lax.all_to_all(all_query_grads, 'head', split_axis=0, concat_axis=1, tile...  5.14 us
    all_to_all x1, starting transfers between devices, per_device(): lax.all_to_all(out_grad, 'head', split_axis=1, concat_axis=0, tiled=True)  3.54 us
    all_to_all x1, starting transfers between devices, per_device(): lax.all_to_all(own_v, 'head', split_axis=0, concat_axis=1, tiled=True)  3.47 us
  transfers between devices with their start and end apart: 10, of which 6 were waited for; matrix products, arithmetic and copies ran while one was open for 17% of the time, Pallas kernels for 0%

profile of v1, /device:TPU:8, one launch (start us, length us, event | category | flops | bytes accessed | tf_op | source)
XLA Modules:
  0.0 94.2 jit_solution(2533710951645964501)
XLA Ops:
  0.6 6.1 %all_gather.7 = bf16[1024,128]{1,0:T(8,128)(2,1)S(1)} all-gather(bf16[256,128]{1,0:T(8,128)(2,1)} %param.19), channel_id=1, replica_groups=mesh['seq'=8,'head'=4] {'head'}, dimensions={0}, use_global_device_ids=true | all-gather | bytes 327680 | tf_op jit(solution)/shard_map/all_gather | solution.py:80
  6.8 3.5 %collective-permute-start.1 = (bf16[64,128]{1,0:T(8,128)(2,1)S(1)}, bf16[64,128]{1,0:T(8,128)(2,1)S(1)}, u32[]{:S(2)}, u32[]{:S(2)}) collective-permute-start(bf16[64,128]{1,0:T(8,128)(2,1)S(1)} %slice_bitcast_fusion.2), channel_id=1, source_target_pairs={{0,4},{4,8},{8,12},{12,16},{16,20},{20,24},{24,28},{1,5},{5,9},{9,... | collective-permute-start | bytes 49160 | tf_op jit(solution)/shard_map/ppermute | solution.py:16
  10.3 5.8 %all_gather.6 = bf16[1024,128]{1,0:T(8,128)(2,1)S(1)} all-gather(bf16[256,128]{1,0:T(8,128)(2,1)S(1)} %copy-done.2), channel_id=1, replica_groups=mesh['seq'=8,'head'=4] {'head'}, dimensions={0}, use_global_device_ids=true | all-gather | bytes 327680 | tf_op jit(solution)/shard_map/all_gather | solution.py:79
  16.1 3.4 %collective-permute-start = (bf16[64,128]{1,0:T(8,128)(2,1)S(1)}, bf16[64,128]{1,0:T(8,128)(2,1)S(1)}, u32[]{:S(2)}, u32[]{:S(2)}) collective-permute-start(bf16[64,128]{1,0:T(8,128)(2,1)S(1)} %slice_bitcast_fusion.3), channel_id=1, source_target_pairs={{0,4},{4,8},{8,12},{12,16},{16,20},{20,24},{24,28},{1,5},{5,9},{9,... | collective-permute-start | bytes 49160 | tf_op jit(solution)/shard_map/ppermute | solution.py:16
  20.6 3.5 %all-to-all-start.2 = ((bf16[256,4,128]{2,0,1:T(8,128)(2,1)}), bf16[256,4,128]{2,0,1:T(8,128)(2,1)S(1)}, u32[]{:S(2)}, u32[]{:S(2)}) async-start(bf16[256,4,128]{2,0,1:T(8,128)(2,1)} %copy.13), calls=%async_computation.2 | async-start | bytes 524288 | tf_op jit(solution)/shard_map/all_to_all | solution.py:76
  26.9 3.2 %all-to-all-done.2 = bf16[256,4,128]{2,0,1:T(8,128)(2,1)S(1)} async-done(((bf16[256,4,128]{2,0,1:T(8,128)(2,1)}), bf16[256,4,128]{2,0,1:T(8,128)(2,1)S(1)}, u32[]{:S(2)}, u32[]{:S(2)}) %all-to-all-start.2) | async-done | bytes 262176 | tf_op jit(solution)/shard_map/all_to_all | solution.py:76
  30.1 3.4 %all-to-all-start = ((bf16[256,4,128]{2,0,1:T(8,128)(2,1)}), bf16[256,4,128]{2,0,1:T(8,128)(2,1)S(1)}, u32[]{:S(2)}, u32[]{:S(2)}) async-start(bf16[256,4,128]{2,0,1:T(8,128)(2,1)} %copy.10), calls=%async_computation | async-start | bytes 524288 | tf_op jit(solution)/shard_map/all_to_all | solution.py:75
  34.0 5.5 %all-to-all-done = bf16[256,4,128]{2,0,1:T(8,128)(2,1)S(1)} async-done(((bf16[256,4,128]{2,0,1:T(8,128)(2,1)}), bf16[256,4,128]{2,0,1:T(8,128)(2,1)S(1)}, u32[]{:S(2)}, u32[]{:S(2)}) %all-to-all-start) | async-done | bytes 262176 | tf_op jit(solution)/shard_map/all_to_all | solution.py:75
  40.7 1.3 %fusion.43 = f32[4,192,128]{2,1,0:T(8,128)} fusion(bf16[4,256,128]{2,1,0:T(8,128)(2,1)S(1)} %bitcast.71, f32[4,128]{1,0:T(4,128)S(1)} %get-tuple-element.74, bf16[4,256,128]{2,1,0:T(8,128)(2,1)S(1)} %bitcast.91, bf16[4,256,128]{2,1,0:T(8,128)(2,1)S(1)} %bitcast.83, bf16[3,64,128]{2,1,0:T(8,128)(2,1)S(1)} %slice.168, bf16[1,64,128]{2,1,0:T(8,128)(2,1)S(1)} %bitcast.105, ...), kind=kOutput, calls=%fused_computation.65 | convolution fusion | flops 53084864 | bytes 1040384 | tf_op jit(solution)/shard_map/dot_general | solution.py:60
  42.0 1.5 %fusion.103 = (f32[4,128]{1,0:T(4,128)S(1)}, f32[4,128,320]{1,2,0:T(8,128)}) fusion(bf16[4,256,128]{2,1,0:T(8,128)(2,1)S(1)} %bitcast.84, bf16[3,64,128]{2,1,0:T(8,128)(2,1)S(1)} %slice.168, bf16[1,64,128]{2,1,0:T(8,128)(2,1)S(1)} %bitcast.106, bf16[4,256,128]{2,1,0:T(8,128)(2,1)S(1)} %bitcast.92, pred[4]{0:T(512)(128)(4,1)S(1)} %add_compare_fusion, ...), kind=kOutput, calls=%fused_computation.111 | convolution fusion | flops 46367040 | bytes 1207296 | tf_op jit(solution)/shard_map/sub | solution.py:43
  45.3 3.4 %all-to-all-start.1 = ((bf16[4,256,128]{2,1,0:T(8,128)(2,1)}), bf16[4,256,128]{2,1,0:T(8,128)(2,1)S(1)}, u32[]{:S(2)}, u32[]{:S(2)}) async-start(bf16[4,256,128]{2,1,0:T(8,128)(2,1)} %pad_maximum_fusion.4), calls=%async_computation.1 | async-start | bytes 524288 | tf_op jit(solution)/shard_map/all_to_all | solution.py:148
  48.7 1.7 %convolution_convert_fusion = bf16[4,128,128]{2,1,0:T(8,128)(2,1)S(1)} fusion(f32[4,128,320]{1,2,0:T(8,128)S(1)} %convolution_bitcast_fusion, bf16[4,256,128]{2,1,0:T(8,128)(2,1)S(1)} %bitcast.86, bf16[3,64,128]{2,1,0:T(8,128)(2,1)S(1)} %slice.168, bf16[1,64,128]{2,1,0:T(8,128)(2,1)S(1)} %bitcast.108, f32[4,128,320]{1,2,0:T(8,128)} %get-tuple-element.73, ...), kind=kOutput, calls=%fused_computation.28 | convolution fusion | flops 44139328 | bytes 1771520 | tf_op jit(solution)/shard_map/dot_general | solution.py:54
  50.4 1.0 %fusion.22 = f32[4,192,128]{2,1,0:T(8,128)} fusion(f32[4,128,192]{1,2,0:T(8,128)S(1)} %convolution_bitcast_fusion.1, bf16[4,256,128]{2,1,0:T(8,128)(2,1)S(1)} %bitcast.94, f32[4,128,192]{1,2,0:T(8,128)S(1)} %get-tuple-element.75, f32[4,128]{1,0:T(4,128)S(1)} %get-tuple-element.74), kind=kOutput, calls=%fused_computation.32 | convolution fusion | flops 25854656 | bytes 2101248 | tf_op jit(solution)/shard_map/dot_general | solution.py:57
  51.4 1.7 %convolution_add_fusion.1 = f32[4,320,128]{2,1,0:T(8,128)S(1)} fusion(f32[4,128,320]{1,2,0:T(8,128)S(1)} %convolution_bitcast_fusion, f32[4,192,128]{2,1,0:T(8,128)} %fusion.22, bf16[4,256,128]{2,1,0:T(8,128)(2,1)S(1)} %bitcast.95, f32[4,128,320]{1,2,0:T(8,128)} %get-tuple-element.73, f32[4,128]{1,0:T(4,128)S(1)} %get-tuple-element.72), kind=kOutput, calls=%fused_computation.11 | convolution fusion | flops 43254592 | bytes 3805184 | tf_op jit(solution)/shard_map/dot_general | solution.py:57
  53.2 3.3 %collective-permute-start.2 = (f32[64,128]{1,0:T(8,128)S(1)}, f32[64,128]{1,0:T(8,128)S(1)}, u32[]{:S(2)}, u32[]{:S(2)}) collective-permute-start(f32[64,128]{1,0:T(8,128)S(1)} %slice_bitcast_fusion.1), channel_id=1, source_target_pairs={{4,0},{8,4},{12,8},{16,12},{20,16},{24,20},{28,24},{5,1},{9,5},{13... | collective-permute-start | bytes 98312 | tf_op jit(solution)/shard_map/ppermute | solution.py:16
  56.6 1.9 %convolution_add_fusion = f32[4,320,128]{2,1,0:T(8,128)S(1)} fusion(f32[4,192,128]{2,1,0:T(8,128)} %fusion.43, bf16[4,256,128]{2,1,0:T(8,128)(2,1)S(1)} %bitcast.72, f32[4,128]{1,0:T(4,128)S(1)} %get-tuple-element.72, bf16[4,256,128]{2,1,0:T(8,128)(2,1)S(1)} %bitcast.87, bf16[3,64,128]{2,1,0:T(8,128)(2,1)S(1)} %copy-done.4, ...), kind=kOutput, calls=%fused_computation.10 | convolution fusion | flops 88638272 | bytes 1731584 | tf_op jit(solution)/shard_map/dot_general | solution.py:60
  59.6 3.4 %all-to-all-start.3 = ((bf16[4,256,128]{2,1,0:T(8,128)(2,1)}), bf16[4,256,128]{2,1,0:T(8,128)(2,1)S(1)}, u32[]{:S(2)}, u32[]{:S(2)}) async-start(bf16[4,256,128]{2,1,0:T(8,128)(2,1)} %pad_maximum_fusion.5), calls=%async_computation.3 | async-start | bytes 524288 | tf_op jit(solution)/shard_map/all_to_all | solution.py:156
  63.9 5.1 %all-to-all-done.3 = bf16[4,256,128]{2,1,0:T(8,128)(2,1)S(1)} async-done(((bf16[4,256,128]{2,1,0:T(8,128)(2,1)}), bf16[4,256,128]{2,1,0:T(8,128)(2,1)S(1)}, u32[]{:S(2)}, u32[]{:S(2)}) %all-to-all-start.3) | async-done | bytes 262176 | tf_op jit(solution)/shard_map/all_to_all | solution.py:156
  69.0 3.5 %all-to-all-start.4 = ((f32[4,256,128]{2,1,0:T(8,128)}), f32[4,256,128]{2,1,0:T(8,128)S(1)}, u32[]{:S(2)}, u32[]{:S(2)}) async-start(f32[4,256,128]{2,1,0:T(8,128)} %pad_maximum_fusion), calls=%async_computation.4 | async-start | bytes 1048576 | tf_op jit(solution)/shard_map/all_to_all | solution.py:159
  72.5 2.4 %collective-permute-start.3 = (f32[64,128]{1,0:T(8,128)S(1)}, f32[64,128]{1,0:T(8,128)S(1)}, u32[]{:S(2)}, u32[]{:S(2)}) collective-permute-start(f32[64,128]{1,0:T(8,128)S(1)} %slice_bitcast_fusion), channel_id=1, source_target_pairs={{4,0},{8,4},{12,8},{16,12},{20,16},{24,20},{28,24},{5,1},{9,5},{13... | collective-permute-start | bytes 98312 | tf_op jit(solution)/shard_map/ppermute | solution.py:16
  75.0 3.3 %collective-permute-done.3 = f32[64,128]{1,0:T(8,128)S(1)} collective-permute-done((f32[64,128]{1,0:T(8,128)S(1)}, f32[64,128]{1,0:T(8,128)S(1)}, u32[]{:S(2)}, u32[]{:S(2)}) %collective-permute-start.3) | collective-permute-done | bytes 32800 | tf_op jit(solution)/shard_map/ppermute | solution.py:16
  79.2 2.1 %all-to-all-done.4 = f32[4,256,128]{2,1,0:T(8,128)S(1)} async-done(((f32[4,256,128]{2,1,0:T(8,128)}), f32[4,256,128]{2,1,0:T(8,128)S(1)}, u32[]{:S(2)}, u32[]{:S(2)}) %all-to-all-start.4) | async-done | bytes 524320 | tf_op jit(solution)/shard_map/all_to_all | solution.py:159
  81.3 3.5 %all-to-all-start.5 = ((f32[4,256,128]{2,1,0:T(8,128)}), f32[4,256,128]{2,1,0:T(8,128)S(1)}, u32[]{:S(2)}, u32[]{:S(2)}) async-start(f32[4,256,128]{2,1,0:T(8,128)} %pad_maximum_fusion.1), calls=%async_computation.5 | async-start | bytes 1048576 | tf_op jit(solution)/shard_map/all_to_all | solution.py:160
  87.4 6.2 %all-to-all-done.5 = f32[4,256,128]{2,1,0:T(8,128)S(1)} async-done(((f32[4,256,128]{2,1,0:T(8,128)}), f32[4,256,128]{2,1,0:T(8,128)S(1)}, u32[]{:S(2)}, u32[]{:S(2)}) %all-to-all-start.5) | async-done | bytes 524320 | tf_op jit(solution)/shard_map/all_to_all | solution.py:160
  (73 shorter events, 13.1 us)
Async XLA Ops:
  0.6 9.7 %copy-start.2 = (bf16[256,128]{1,0:T(8,128)(2,1)S(1)}, bf16[256,128]{1,0:T(8,128)(2,1)}, u32[]{:S(2)}) copy-start(bf16[256,128]{1,0:T(8,128)(2,1)} %param.18) | copy-start | bytes 196612
  6.8 12.8 %copy-start = (bf16[256,512]{1,0:T(8,128)(2,1)S(1)}, bf16[256,512]{1,0:T(8,128)(2,1)}, u32[]{:S(2)}) copy-start(bf16[256,512]{1,0:T(8,128)(2,1)} %param.20) | copy-start | bytes 786436
  6.8 26.7 %collective-permute-start.1 = (bf16[64,128]{1,0:T(8,128)(2,1)S(1)}, bf16[64,128]{1,0:T(8,128)(2,1)S(1)}, u32[]{:S(2)}, u32[]{:S(2)}) collective-permute-start(bf16[64,128]{1,0:T(8,128)(2,1)S(1)} %slice_bitcast_fusion.2), channel_id=1, source_target_pairs={{0,4},{4,8},{8,12},{12,16},{16,20},{20,24},{24,28},{1,5},{5,9},{9,... | collective-permute-start | bytes 49160 | tf_op jit(solution)/shard_map/ppermute | solution.py:16
  16.1 17.9 %collective-permute-start = (bf16[64,128]{1,0:T(8,128)(2,1)S(1)}, bf16[64,128]{1,0:T(8,128)(2,1)S(1)}, u32[]{:S(2)}, u32[]{:S(2)}) collective-permute-start(bf16[64,128]{1,0:T(8,128)(2,1)S(1)} %slice_bitcast_fusion.3), channel_id=1, source_target_pairs={{0,4},{4,8},{8,12},{12,16},{16,20},{20,24},{24,28},{1,5},{5,9},{9,... | collective-permute-start | bytes 49160 | tf_op jit(solution)/shard_map/ppermute | solution.py:16
  20.5 3.7 %copy-start.8 = (s32[32]{0:T(128)S(1)}, s32[32]{0:T(128)}, u32[]{:S(2)}) copy-start(s32[32]{0:T(128)} %param.21) | copy-start | bytes 388
  20.6 9.5 %all-to-all-start.2 = ((bf16[256,4,128]{2,0,1:T(8,128)(2,1)}), bf16[256,4,128]{2,0,1:T(8,128)(2,1)S(1)}, u32[]{:S(2)}, u32[]{:S(2)}) async-start(bf16[256,4,128]{2,0,1:T(8,128)(2,1)} %copy.13), calls=%async_computation.2 | async-start | bytes 524288 | tf_op jit(solution)/shard_map/all_to_all | solution.py:76
  24.1 1.8 %copy-start.1 = (bf16[256,512]{1,0:T(8,128)(2,1)S(1)}, bf16[256,512]{1,0:T(8,128)(2,1)}, u32[]{:S(2)}) copy-start(bf16[256,512]{1,0:T(8,128)(2,1)} %param.17) | copy-start | bytes 786436
  24.1 19.4 %copy-start.11 = (pred[320]{0:T(512)(128)(4,1)}, pred[320]{0:T(512)(128)(4,1)S(1)}, u32[]{:S(2)}) copy-start(pred[320]{0:T(512)(128)(4,1)S(1)} %broadcast_compare_fusion.1) | copy-start | bytes 964
  24.2 19.4 %copy-start.9 = (pred[4]{0:T(512)(128)(4,1)}, pred[4]{0:T(512)(128)(4,1)S(1)}, u32[]{:S(2)}) copy-start(pred[4]{0:T(512)(128)(4,1)S(1)} %add_compare_fusion) | copy-start | bytes 16
  25.1 18.5 %copy-start.5 = (pred[128,320]{0,1:T(8,128)(4,1)}, pred[128,320]{0,1:T(8,128)(4,1)S(1)}, u32[]{:S(2)}) copy-start(pred[128,320]{0,1:T(8,128)(4,1)S(1)} %broadcast_compare_fusion) | copy-start | bytes 122884
  25.9 22.8 %copy-start.3 = (bf16[3,64,128]{2,1,0:T(8,128)(2,1)}, bf16[3,64,128]{2,1,0:T(8,128)(2,1)S(1)}, u32[]{:S(2)}) copy-start(bf16[3,64,128]{2,1,0:T(8,128)(2,1)S(1)} %slice.168) | copy-start | bytes 147460
  30.1 9.4 %all-to-all-start = ((bf16[256,4,128]{2,0,1:T(8,128)(2,1)}), bf16[256,4,128]{2,0,1:T(8,128)(2,1)S(1)}, u32[]{:S(2)}, u32[]{:S(2)}) async-start(bf16[256,4,128]{2,0,1:T(8,128)(2,1)} %copy.10), calls=%async_computation | async-start | bytes 524288 | tf_op jit(solution)/shard_map/all_to_all | solution.py:75
  34.0 14.7 %copy-start.6 = (bf16[64,128]{1,0:T(8,128)(2,1)}, bf16[64,128]{1,0:T(8,128)(2,1)S(1)}, u32[]{:S(2)}) copy-start(bf16[64,128]{1,0:T(8,128)(2,1)S(1)} %collective-permute-done) | copy-start | bytes 49156
  45.3 14.3 %all-to-all-start.1 = ((bf16[4,256,128]{2,1,0:T(8,128)(2,1)}), bf16[4,256,128]{2,1,0:T(8,128)(2,1)S(1)}, u32[]{:S(2)}, u32[]{:S(2)}) async-start(bf16[4,256,128]{2,1,0:T(8,128)(2,1)} %pad_maximum_fusion.4), calls=%async_computation.1 | async-start | bytes 524288 | tf_op jit(solution)/shard_map/all_to_all | solution.py:148
  51.4 5.1 %copy-start.10 = (pred[4]{0:T(512)(128)(4,1)S(1)}, pred[4]{0:T(512)(128)(4,1)}, u32[]{:S(2)}) copy-start(pred[4]{0:T(512)(128)(4,1)} %copy-done.9) | copy-start | bytes 16
  51.4 5.1 %copy-start.12 = (pred[320]{0:T(512)(128)(4,1)S(1)}, pred[320]{0:T(512)(128)(4,1)}, u32[]{:S(2)}) copy-start(pred[320]{0:T(512)(128)(4,1)} %copy-done.11) | copy-start | bytes 964
  53.2 3.4 %copy-start.4 = (bf16[3,64,128]{2,1,0:T(8,128)(2,1)S(1)}, bf16[3,64,128]{2,1,0:T(8,128)(2,1)}, u32[]{:S(2)}) copy-start(bf16[3,64,128]{2,1,0:T(8,128)(2,1)} %copy-done.3) | copy-start | bytes 147460
  53.2 3.4 %copy-start.7 = (bf16[64,128]{1,0:T(8,128)(2,1)S(1)}, bf16[64,128]{1,0:T(8,128)(2,1)}, u32[]{:S(2)}) copy-start(bf16[64,128]{1,0:T(8,128)(2,1)} %copy-done.6) | copy-start | bytes 49156
  53.2 9.8 %collective-permute-start.2 = (f32[64,128]{1,0:T(8,128)S(1)}, f32[64,128]{1,0:T(8,128)S(1)}, u32[]{:S(2)}, u32[]{:S(2)}) collective-permute-start(f32[64,128]{1,0:T(8,128)S(1)} %slice_bitcast_fusion.1), channel_id=1, source_target_pairs={{4,0},{8,4},{12,8},{16,12},{20,16},{24,20},{28,24},{5,1},{9,5},{13... | collective-permute-start | bytes 98312 | tf_op jit(solution)/shard_map/ppermute | solution.py:16
  59.6 9.4 %all-to-all-start.3 = ((bf16[4,256,128]{2,1,0:T(8,128)(2,1)}), bf16[4,256,128]{2,1,0:T(8,128)(2,1)S(1)}, u32[]{:S(2)}, u32[]{:S(2)}) async-start(bf16[4,256,128]{2,1,0:T(8,128)(2,1)} %pad_maximum_fusion.5), calls=%async_computation.3 | async-start | bytes 524288 | tf_op jit(solution)/shard_map/all_to_all | solution.py:156
  69.0 12.3 %all-to-all-start.4 = ((f32[4,256,128]{2,1,0:T(8,128)}), f32[4,256,128]{2,1,0:T(8,128)S(1)}, u32[]{:S(2)}, u32[]{:S(2)}) async-start(f32[4,256,128]{2,1,0:T(8,128)} %pad_maximum_fusion), calls=%async_computation.4 | async-start | bytes 1048576 | tf_op jit(solution)/shard_map/all_to_all | solution.py:159
  72.5 5.8 %collective-permute-start.3 = (f32[64,128]{1,0:T(8,128)S(1)}, f32[64,128]{1,0:T(8,128)S(1)}, u32[]{:S(2)}, u32[]{:S(2)}) collective-permute-start(f32[64,128]{1,0:T(8,128)S(1)} %slice_bitcast_fusion), channel_id=1, source_target_pairs={{4,0},{8,4},{12,8},{16,12},{20,16},{24,20},{28,24},{5,1},{9,5},{13... | collective-permute-start | bytes 98312 | tf_op jit(solution)/shard_map/ppermute | solution.py:16
  81.3 12.3 %all-to-all-start.5 = ((f32[4,256,128]{2,1,0:T(8,128)}), f32[4,256,128]{2,1,0:T(8,128)S(1)}, u32[]{:S(2)}, u32[]{:S(2)}) async-start(f32[4,256,128]{2,1,0:T(8,128)} %pad_maximum_fusion.1), calls=%async_computation.5 | async-start | bytes 1048576 | tf_op jit(solution)/shard_map/all_to_all | solution.py:160
